TPU v7x, 256 devices: a whole 4x4x8 slice. The times are simulated.
256 devices in a mesh: row: 32 (over z, y), col: 8 (over x, core).
Axes of the slice: x: 4, y: 4, z: 8, core: 2. Of those that a mesh axis runs over, the one named last changes fastest.
Arguments:
- factor: float32 [32, 3, 1024, 4, 1024], P('row', None, None, None, 'col'), may hold values from -0.01953125 to 0.01953125
- knowns: float32 [32, 3, 1024, 256], P('row'), may hold values from -6 to 6
- inverse: float32 [4, 1024, 1024], P(None, None, 'col'), may hold values from -0.1875 to 0.1875
Outputs:
- solved: float32 [4, 1024, 256], P(None, 'col', 'row')
All inputs are finite; a program needn't handle non-finite values.
Results may differ from a plain program's by a relative error of at most 0.0001.
Values sent between devices are 32-bit elements; how exact they have to be, the bound alone decides.
A program may use at most 64 MiB of HBM per device.

v0:
```python
import jax
import jax.numpy as jnp
from jax import lax
from jax.sharding import PartitionSpec as P

NBLK = 96
KW = 4


def from_root(value, axis, root):
    mine = lax.axis_index(axis) == root
    return lax.psum(jnp.where(mine, value, jnp.zeros_like(value)), axis)


def apply_inverse(residual, inverse_block):
    full_resid = lax.all_gather(residual, "col", axis=0, tiled=True)
    return jnp.einsum(
        "cm,cs->ms",
        inverse_block,
        full_resid,
        precision=lax.Precision.HIGHEST,
        preferred_element_type=jnp.float32,
    )


def spread_block(own_factor, local_slot, solved_part):
    rows_block = own_factor[local_slot]
    return jnp.einsum(
        "ajc,as->jcs",
        rows_block,
        lax.all_gather(solved_part, "col", axis=0, tiled=True),
        precision=lax.Precision.HIGHEST,
        preferred_element_type=jnp.float32,
    )


def own_sources(stacked, row_index, row_count):
    source_width = stacked.shape[2] // row_count
    return lax.dynamic_slice_in_dim(stacked, row_index * source_width, source_width, 2)


def on_device(factor, knowns, inverse):
    row_count = lax.axis_size("row")
    row_index = lax.axis_index("row")
    col_index = lax.axis_index("col")
    slice_width = factor.shape[4]
    first_block = NBLK - KW
    own_factor = factor[0]
    own_knowns = knowns[0]
    counted = lax.iota(jnp.int32, own_knowns.shape[0]) * row_count + row_index
    keep_mask = (counted < first_block).astype(jnp.float32)
    prefix = jnp.einsum(
        "lajc,las->jcs",
        own_factor,
        own_knowns * keep_mask[:, None, None],
        precision=lax.Precision.HIGHEST,
        preferred_element_type=jnp.float32,
    )
    owned_rhs = []
    for step in range(KW):
        block_id = first_block + step
        rhs_slice = lax.dynamic_slice_in_dim(
            own_knowns[block_id // row_count], col_index * slice_width, slice_width, 0
        )
        owner_mask = (row_index == block_id % row_count).astype(jnp.float32)
        owned_rhs.append(owner_mask * rhs_slice)
    local_terms = prefix - jnp.stack(owned_rhs)
    correction = jnp.zeros_like(local_terms)
    solved_parts = []
    totals = lax.psum(local_terms, "row")
    for step in range(KW):
        block_id = first_block + step
        residual = -(totals[step] + correction[step])
        solved_part = apply_inverse(residual, inverse[step])
        solved_parts.append(solved_part)
        if step + 1 < KW:
            contrib = spread_block(own_factor, block_id // row_count, solved_part)
            correction = correction + from_root(contrib, "row", block_id % row_count)
    return own_sources(jnp.stack(solved_parts), row_index, row_count)


def solution(mesh):
    return jax.shard_map(
        on_device,
        mesh=mesh,
        in_specs=(
            P("row", None, None, None, "col"),
            P("row", None, None, None),
            P(None, None, "col"),
        ),
        out_specs=P(None, "col", "row"),
        check_vma=False,
    )
```

profile of v0, /device:TPU:1, one launch (start us, length us, event | category | flops | bytes accessed | tf_op | source)
XLA Modules:
  0.0 832.3 jit_solution(10658403784603572605)
XLA Ops:
  7.9 10.2 %fusion.18 = f32[4,128,256]{1,2,0:T(8,128)} fusion(f32[3,1024,4,128]{3,2,1,0:T(4,128)} %bitcast.101, f32[1,3,1024,256]{3,2,1,0:T(8,128)} %param.4, f32[3]{0:T(128)S(1)} %compare_convert_fusion, f32[1,128,256]{1,2,0:T(8,128)S(1)} %get-tuple-element.6, f32[1,128,256]{1,2,0:T(8,128)S(1)} %get-tuple-element.7, f32[1,128,256]{1,2,0:T(8,128)S(1)} %get-tuple-element.8, ...), kind=kOutput, calls=%fused_computation.16 | convolution fusion | flops 4833148928 | bytes 10485772 | tf_op jit(solution)/shard_map/lajc,las->jcs/dot_general | solution.py:52
  18.2 148.2 %all-reduce.5.cloned.1.call-done = f32[4,128,256]{1,2,0:T(8,128)} async-done(((f32[4,128,256]{1,2,0:T(8,128)}), f32[4,128,256]{1,2,0:T(8,128)}) %all-reduce.5.cloned.1.call-update) | async-done | bytes 524304 | tf_op jit(solution)/shard_map/psum | solution.py:70
  166.4 1.6 slice_negate_fusion
  168.0 27.9 %all-gather.18.cloned.1.call-done = f32[1,1024,256]{1,2,0:T(8,128)} async-done(((f32[1,128,256]{1,2,0:T(8,128)}), f32[1,1024,256]{1,2,0:T(8,128)}) %all-gather.18.cloned.1.call-update) | async-done | bytes 1048592 | tf_op jit(solution)/shard_map/all_gather | solution.py:16
  195.9 3.0 fusion.31
  199.0 1.7 slice.50
  200.8 25.2 %all-gather.12.cloned.1.call-done = f32[1024,256]{0,1:T(8,128)} async-done(((f32[128,256]{0,1:T(8,128)}), f32[1024,256]{0,1:T(8,128)}) %all-gather.12.cloned.1.call-update) | async-done | bytes 1048592 | tf_op jit(solution)/shard_map/all_gather | solution.py:31
  225.9 4.0 fusion.13
  230.0 145.1 %all-reduce.7.cloned.1.call-done = f32[4,128,256]{1,2,0:T(8,128)} async-done(((f32[4,128,256]{1,2,0:T(8,128)}), f32[4,128,256]{1,2,0:T(8,128)}) %all-reduce.7.cloned.1.call-update) | async-done | bytes 524304 | tf_op jit(solution)/shard_map/psum | solution.py:12
  375.0 1.6 fusion.44
  376.7 27.8 %all-gather.20.cloned.1.call-done = f32[1,1024,256]{1,2,0:T(8,128)} async-done(((f32[1,128,256]{1,2,0:T(8,128)}), f32[1,1024,256]{1,2,0:T(8,128)}) %all-gather.20.cloned.1.call-update) | async-done | bytes 1048592 | tf_op jit(solution)/shard_map/all_gather | solution.py:16
  404.5 3.0 fusion.28
  407.8 26.7 %all-gather.14.cloned.1.call-done = f32[1024,256]{0,1:T(8,128)} async-done(((f32[128,256]{0,1:T(8,128)}), f32[1024,256]{0,1:T(8,128)}) %all-gather.14.cloned.1.call-update) | async-done | bytes 1048592 | tf_op jit(solution)/shard_map/all_gather | solution.py:31
  434.5 4.0 fusion.15
  438.5 145.1 %all-reduce.9.cloned.1.call-done = f32[4,128,256]{1,2,0:T(8,128)} async-done(((f32[4,128,256]{1,2,0:T(8,128)}), f32[4,128,256]{1,2,0:T(8,128)}) %all-reduce.9.cloned.1.call-update) | async-done | bytes 524304 | tf_op jit(solution)/shard_map/psum | solution.py:12
  584.7 1.6 fusion.43
  586.4 27.8 %all-gather.22.cloned.1.call-done = f32[1,1024,256]{1,2,0:T(8,128)} async-done(((f32[1,128,256]{1,2,0:T(8,128)}), f32[1,1024,256]{1,2,0:T(8,128)}) %all-gather.22.cloned.1.call-update) | async-done | bytes 1048592 | tf_op jit(solution)/shard_map/all_gather | solution.py:16
  614.2 3.0 fusion.25
  617.2 26.9 %all-gather.16.cloned.1.call-done = f32[1024,256]{0,1:T(8,128)} async-done(((f32[128,256]{0,1:T(8,128)}), f32[1024,256]{0,1:T(8,128)}) %all-gather.16.cloned.1.call-update) | async-done | bytes 1048592 | tf_op jit(solution)/shard_map/all_gather | solution.py:31
  644.1 4.0 fusion.17
  648.1 145.1 %all-reduce.11.cloned.1.call-done = f32[4,128,256]{1,2,0:T(8,128)} async-done(((f32[4,128,256]{1,2,0:T(8,128)}), f32[4,128,256]{1,2,0:T(8,128)}) %all-reduce.11.cloned.1.call-update) | async-done | bytes 524304 | tf_op jit(solution)/shard_map/psum | solution.py:12
  793.2 1.6 fusion.42
  794.9 27.9 %all-gather.24.cloned.1.call-done = f32[1,1024,256]{1,2,0:T(8,128)} async-done(((f32[1,128,256]{1,2,0:T(8,128)}), f32[1,1024,256]{1,2,0:T(8,128)}) %all-gather.24.cloned.1.call-update) | async-done | bytes 1048592 | tf_op jit(solution)/shard_map/all_gather | solution.py:16
  822.7 2.3 convolution_bitcast_fusion
  (38 shorter events, 3.8 us)
Async XLA Ops:
  6.5 1.2 slice-start
  6.5 159.9 %all-reduce.5.cloned.1.call-start = ((), (), s32[]{:S(2)}) async-start(), calls=%async_computation | async-start | bytes 1048576 | tf_op jit(solution)/shard_map/psum | solution.py:70
  18.1 177.8 %all-gather.18.cloned.1.call-start = ((), (), s32[]{:S(2)}) async-start(), calls=%async_computation.7 | async-start | bytes 1179648 | tf_op jit(solution)/shard_map/all_gather | solution.py:16
  168.0 57.9 %all-gather.12.cloned.1.call-start = ((), (), s32[]{:S(2)}) async-start(), calls=%async_computation.1 | async-start | bytes 1179648 | tf_op jit(solution)/shard_map/all_gather | solution.py:31
  199.0 176.0 %all-reduce.7.cloned.1.call-start = ((), (), s32[]{:S(2)}) async-start(), calls=%async_computation.2 | async-start | bytes 1048576 | tf_op jit(solution)/shard_map/psum | solution.py:12
  229.9 174.6 %all-gather.20.cloned.1.call-start = ((), (), s32[]{:S(2)}) async-start(), calls=%async_computation.8 | async-start | bytes 1179648 | tf_op jit(solution)/shard_map/all_gather | solution.py:16
  376.7 57.8 %all-gather.14.cloned.1.call-start = ((), (), s32[]{:S(2)}) async-start(), calls=%async_computation.3 | async-start | bytes 1179648 | tf_op jit(solution)/shard_map/all_gather | solution.py:31
  407.5 176.1 %copy-start.3 = (f32[4,128,256]{1,2,0:T(8,128)S(1)}, f32[4,128,256]{1,2,0:T(8,128)}, u32[]{:S(2)}) copy-start(f32[4,128,256]{1,2,0:T(8,128)} %all-reduce.7.cloned.1.call-done) | copy-start | bytes 1572868
  407.5 176.1 %all-reduce.9.cloned.1.call-start = ((), (), s32[]{:S(2)}) async-start(), calls=%async_computation.4 | async-start | bytes 1048576 | tf_op jit(solution)/shard_map/psum | solution.py:12
  438.5 175.7 %all-gather.22.cloned.1.call-start = ((), (), s32[]{:S(2)}) async-start(), calls=%async_computation.9 | async-start | bytes 1179648 | tf_op jit(solution)/shard_map/all_gather | solution.py:16
  586.3 57.8 %all-gather.16.cloned.1.call-start = ((), (), s32[]{:S(2)}) async-start(), calls=%async_computation.5 | async-start | bytes 1179648 | tf_op jit(solution)/shard_map/all_gather | solution.py:31
  617.2 176.0 %all-reduce.11.cloned.1.call-start = ((), (), s32[]{:S(2)}) async-start(), calls=%async_computation.6 | async-start | bytes 1048576 | tf_op jit(solution)/shard_map/psum | solution.py:12
  648.1 177.0 %copy-start = (f32[256,128]{1,0:T(8,128)S(1)}, f32[256,128]{1,0:T(8,128)}, u32[]{:S(2)}) copy-start(f32[256,128]{1,0:T(8,128)} %fusion.31) | copy-start | bytes 393220
  648.1 177.1 %copy-start.1 = (f32[256,128]{1,0:T(8,128)S(1)}, f32[256,128]{1,0:T(8,128)}, u32[]{:S(2)}) copy-start(f32[256,128]{1,0:T(8,128)} %fusion.28) | copy-start | bytes 393220
  648.1 177.1 %copy-start.2 = (f32[256,128]{1,0:T(8,128)S(1)}, f32[256,128]{1,0:T(8,128)}, u32[]{:S(2)}) copy-start(f32[256,128]{1,0:T(8,128)} %fusion.25) | copy-start | bytes 393220
  648.1 174.7 %all-gather.24.cloned.1.call-start = ((), (), s32[]{:S(2)}) async-start(), calls=%async_computation.10 | async-start | bytes 1179648 | tf_op jit(solution)/shard_map/all_gather | solution.py:16
Sparse Core Ops, SparseCore 0:
  18.2 148.1 all-reduce.4
  168.2 27.6 all-gather.17
  199.1 26.7 all-gather.11
  230.0 144.9 all-reduce.6
  376.8 27.6 all-gather.19
  407.7 26.7 all-gather.13
  438.6 144.9 all-reduce.8
  586.4 27.6 all-gather.21
  617.3 26.7 all-gather.15
  648.2 144.9 all-reduce.10
  795.0 27.6 all-gather.23
where the time goes:
time: 833 us; the launch traced here: 832 us
  waiting for transfers between devices  774 us (93%)
  matrix products  33.4 us (4%)
  between operations  13.3 us (2%)
    psum x3, waiting for transfers between devices, from_root(): return lax.psum(jnp.where(mine, value, jnp.zeros_like(value)), axis)  435 us
    psum x1, waiting for transfers between devices, on_device(): totals = lax.psum(local_terms, 'row')  148 us
    all_gather x4, waiting for transfers between devices, apply_inverse(): full_resid = lax.all_gather(residual, 'col', axis=0, tiled=True)  111 us
    all_gather x3, waiting for transfers between devices, spread_block(): lax.all_gather(solved_part, 'col', axis=0, tiled=True)  78.7 us
  transfers between devices with their start and end apart: 11, of which 11 were waited for; matrix products, arithmetic and copies ran while one was open for 0% of the time, Pallas kernels for 0%

commit v1 on v0

--- a/solution.py
+++ b/solution.py
@@ -7,13 +7,18 @@
 KW = 4
 
 
+def swapped_in(x, name, dim):
+    outgoing = jnp.stack([x] * lax.axis_size(name))
+    return jnp.concatenate(lax.all_to_all(outgoing, name, 0, 0), axis=dim)
+
+
 def from_root(value, axis, root):
     mine = lax.axis_index(axis) == root
     return lax.psum(jnp.where(mine, value, jnp.zeros_like(value)), axis)
 
 
 def apply_inverse(residual, inverse_block):
-    full_resid = lax.all_gather(residual, "col", axis=0, tiled=True)
+    full_resid = swapped_in(residual, "col", 0)
     return jnp.einsum(
         "cm,cs->ms",
         inverse_block,

time: 833 us -> 805 us (0.966)
  waiting for transfers between devices: 774 us -> 662 us
  blocking collectives: 0 us -> 72.5 us
  starting transfers between devices: 0.6 us -> 9.81 us
    all_gather x4 -> x0, waiting for transfers between devices: 111 us -> none  [apply_inverse(): full_resid = lax.all_gather(residual, 'col', axis=0, tiled=True)]
    all_to_all x0 -> x3, blocking collectives: none -> 72.5 us  [swapped_in(): return jnp.concatenate(lax.all_to_all(outgoing, name, 0, 0), axis=dim)]
    all_to_all x0 -> x1, waiting for transfers between devices: none -> 15 us  [swapped_in(): return jnp.concatenate(lax.all_to_all(outgoing, name, 0, 0), axis=dim)]
    all_gather x3, waiting for transfers between devices: 78.7 us -> 63.8 us  [spread_block(): lax.all_gather(solved_part, 'col', axis=0, tiled=True)]
    all_to_all x0 -> x1, starting transfers between devices: none -> 9.55 us  [swapped_in(): return jnp.concatenate(lax.all_to_all(outgoing, name, 0, 0), axis=dim)]
  transfers between devices with their start and end apart: 11 -> 8, of which waited for: 11 -> 8; matrix products, arithmetic and copies ran while one was open for 0% -> 0% of each run, Pallas kernels for 0% -> 0%
where the time goes in v1:
time: 805 us; the launch traced here: 804 us
  waiting for transfers between devices  662 us (82%)
  blocking collectives  72.5 us (9%)
  matrix products  35.4 us (4%)
  between operations  13.6 us (2%)
  starting transfers between devices  9.81 us (1%)
    psum x3, waiting for transfers between devices, from_root(): return lax.psum(jnp.where(mine, value, jnp.zeros_like(value)), axis)  435 us
    psum x1, waiting for transfers between devices, on_device(): totals = lax.psum(local_terms, 'row')  148 us
    all_to_all x3, blocking collectives, swapped_in(): return jnp.concatenate(lax.all_to_all(outgoing, name, 0, 0), axis=dim)  72.5 us
    all_gather x3, waiting for transfers between devices, spread_block(): lax.all_gather(solved_part, 'col', axis=0, tiled=True)  63.8 us
  transfers between devices with their start and end apart: 8, of which 8 were waited for; matrix products, arithmetic and copies ran while one was open for 0% of the time, Pallas kernels for 0%

profile of v1, /device:TPU:1, one launch (start us, length us, event | category | flops | bytes accessed | tf_op | source)
XLA Modules:
  0.0 803.9 jit_solution(721271304580330231)
XLA Ops:
  6.6 1.2 slice-done
  7.9 10.2 %fusion.18 = f32[4,128,256]{1,2,0:T(8,128)} fusion(f32[3,1024,4,128]{3,2,1,0:T(4,128)} %bitcast.105, f32[1,3,1024,256]{3,2,1,0:T(8,128)} %param.4, f32[3]{0:T(128)S(1)} %compare_convert_fusion, f32[1,128,256]{1,2,0:T(8,128)S(1)} %get-tuple-element.6, f32[1,128,256]{1,2,0:T(8,128)S(1)} %get-tuple-element.7, f32[1,128,256]{1,2,0:T(8,128)S(1)} %get-tuple-element.8, ...), kind=kOutput, calls=%fused_computation.16 | convolution fusion | flops 4833148928 | bytes 10485772 | tf_op jit(solution)/shard_map/lajc,las->jcs/dot_general | solution.py:57
  18.2 148.2 %all-reduce.5.cloned.1.call-done = f32[4,128,256]{1,2,0:T(8,128)} async-done(((f32[4,128,256]{1,2,0:T(8,128)}), f32[4,128,256]{1,2,0:T(8,128)}) %all-reduce.5.cloned.1.call-update) | async-done | bytes 524304 | tf_op jit(solution)/shard_map/psum | solution.py:75
  167.5 24.2 %all_to_all.20 = f32[8,128,256]{2,1,0:T(8,128)S(1)} all-to-all(f32[8,128,256]{2,1,0:T(8,128)S(1)} %stack.30), channel_id=1, replica_groups=mesh['row'=32,'col'=8] {'col'}, dimensions={0} | all-to-all | bytes 2097152 | tf_op jit(solution)/shard_map/all_to_all | solution.py:12
  191.7 3.5 fusion.31
  195.2 1.7 slice.50
  197.0 20.1 %all-gather.4.cloned.1.call-done = f32[1024,256]{0,1:T(8,128)} async-done(((f32[128,256]{0,1:T(8,128)}), f32[1024,256]{0,1:T(8,128)}) %all-gather.4.cloned.1.call-update) | async-done | bytes 1048592 | tf_op jit(solution)/shard_map/all_gather | solution.py:36
  217.1 4.0 fusion.13
  221.1 145.1 %all-reduce.7.cloned.1.call-done = f32[4,128,256]{1,2,0:T(8,128)} async-done(((f32[4,128,256]{1,2,0:T(8,128)}), f32[4,128,256]{1,2,0:T(8,128)}) %all-reduce.7.cloned.1.call-update) | async-done | bytes 524304 | tf_op jit(solution)/shard_map/psum | solution.py:17
  367.3 24.2 %all_to_all.21 = f32[8,128,256]{2,1,0:T(8,128)S(1)} all-to-all(f32[8,128,256]{2,1,0:T(8,128)S(1)} %stack.33), channel_id=1, replica_groups=mesh['row'=32,'col'=8] {'col'}, dimensions={0} | all-to-all | bytes 2097152 | tf_op jit(solution)/shard_map/all_to_all | solution.py:12
  391.5 3.5 fusion.29
  395.1 21.8 %all-gather.6.cloned.1.call-done = f32[1024,256]{0,1:T(8,128)} async-done(((f32[128,256]{0,1:T(8,128)}), f32[1024,256]{0,1:T(8,128)}) %all-gather.6.cloned.1.call-update) | async-done | bytes 1048592 | tf_op jit(solution)/shard_map/all_gather | solution.py:36
  416.9 4.0 fusion.15
  421.0 145.0 %all-reduce.9.cloned.1.call-done = f32[4,128,256]{1,2,0:T(8,128)} async-done(((f32[4,128,256]{1,2,0:T(8,128)}), f32[4,128,256]{1,2,0:T(8,128)}) %all-reduce.9.cloned.1.call-update) | async-done | bytes 524304 | tf_op jit(solution)/shard_map/psum | solution.py:17
  566.0 1.1 add.49
  568.2 24.2 %all_to_all.22 = f32[8,128,256]{2,1,0:T(8,128)S(1)} all-to-all(f32[8,128,256]{2,1,0:T(8,128)S(1)} %stack.36), channel_id=1, replica_groups=mesh['row'=32,'col'=8] {'col'}, dimensions={0} | all-to-all | bytes 2097152 | tf_op jit(solution)/shard_map/all_to_all | solution.py:12
  592.4 3.5 fusion.27
  596.0 21.8 %all-gather.8.cloned.1.call-done = f32[1024,256]{0,1:T(8,128)} async-done(((f32[128,256]{0,1:T(8,128)}), f32[1024,256]{0,1:T(8,128)}) %all-gather.8.cloned.1.call-update) | async-done | bytes 1048592 | tf_op jit(solution)/shard_map/all_gather | solution.py:36
  617.8 4.0 fusion.17
  621.8 145.1 %all-reduce.11.cloned.1.call-done = f32[4,128,256]{1,2,0:T(8,128)} async-done(((f32[4,128,256]{1,2,0:T(8,128)}), f32[4,128,256]{1,2,0:T(8,128)}) %all-reduce.11.cloned.1.call-update) | async-done | bytes 524304 | tf_op jit(solution)/shard_map/psum | solution.py:17
  768.0 1.1 stack.39
  769.1 9.6 %all-to-all-start.3 = ((f32[8,128,256]{2,1,0:T(8,128)}), f32[8,128,256]{2,1,0:T(8,128)S(1)}, u32[]{:S(2)}, u32[]{:S(2)}) async-start(f32[8,128,256]{2,1,0:T(8,128)} %stack.39), calls=%async_computation.3 | async-start | bytes 2097152 | tf_op jit(solution)/shard_map/all_to_all | solution.py:12
  778.6 15.0 %all-to-all-done.3 = f32[8,128,256]{2,1,0:T(8,128)S(1)} async-done(((f32[8,128,256]{2,1,0:T(8,128)}), f32[8,128,256]{2,1,0:T(8,128)S(1)}, u32[]{:S(2)}, u32[]{:S(2)}) %all-to-all-start.3) | async-done | bytes 1048608 | tf_op jit(solution)/shard_map/all_to_all | solution.py:12
  793.6 2.8 convolution_bitcast_fusion
  (39 shorter events, 5.6 us)
Async XLA Ops:
  6.5 1.2 slice-start
  6.5 159.8 %all-reduce.5.cloned.1.call-start = ((), (), s32[]{:S(2)}) async-start(), calls=%async_computation.4 | async-start | bytes 1048576 | tf_op jit(solution)/shard_map/psum | solution.py:75
  18.1 199.0 %all-gather.4.cloned.1.call-start = ((), (), s32[]{:S(2)}) async-start(), calls=%async_computation.5 | async-start | bytes 1179648 | tf_op jit(solution)/shard_map/all_gather | solution.py:36
  195.2 171.0 %all-reduce.7.cloned.1.call-start = ((), (), s32[]{:S(2)}) async-start(), calls=%async_computation.6 | async-start | bytes 1048576 | tf_op jit(solution)/shard_map/psum | solution.py:17
  221.1 195.9 %all-gather.6.cloned.1.call-start = ((), (), s32[]{:S(2)}) async-start(), calls=%async_computation.7 | async-start | bytes 1179648 | tf_op jit(solution)/shard_map/all_gather | solution.py:36
  395.0 171.0 %copy-start.3 = (f32[4,128,256]{1,2,0:T(8,128)S(1)}, f32[4,128,256]{1,2,0:T(8,128)}, u32[]{:S(2)}) copy-start(f32[4,128,256]{1,2,0:T(8,128)} %all-reduce.7.cloned.1.call-done) | copy-start | bytes 1572868
  395.0 171.0 %all-reduce.9.cloned.1.call-start = ((), (), s32[]{:S(2)}) async-start(), calls=%async_computation.8 | async-start | bytes 1048576 | tf_op jit(solution)/shard_map/psum | solution.py:17
  420.9 196.9 %all-gather.8.cloned.1.call-start = ((), (), s32[]{:S(2)}) async-start(), calls=%async_computation.9 | async-start | bytes 1179648 | tf_op jit(solution)/shard_map/all_gather | solution.py:36
  595.9 171.0 %all-reduce.11.cloned.1.call-start = ((), (), s32[]{:S(2)}) async-start(), calls=%async_computation.10 | async-start | bytes 1048576 | tf_op jit(solution)/shard_map/psum | solution.py:17
  769.1 27.4 %copy-start = (f32[256,128]{1,0:T(8,128)S(1)}, f32[256,128]{1,0:T(8,128)}, u32[]{:S(2)}) copy-start(f32[256,128]{1,0:T(8,128)} %fusion.31) | copy-start | bytes 393220
  769.1 27.4 %copy-start.1 = (f32[256,128]{1,0:T(8,128)S(1)}, f32[256,128]{1,0:T(8,128)}, u32[]{:S(2)}) copy-start(f32[256,128]{1,0:T(8,128)} %fusion.29) | copy-start | bytes 393220
  769.1 27.4 %copy-start.2 = (f32[256,128]{1,0:T(8,128)S(1)}, f32[256,128]{1,0:T(8,128)}, u32[]{:S(2)}) copy-start(f32[256,128]{1,0:T(8,128)} %fusion.27) | copy-start | bytes 393220
  769.1 24.5 %all-to-all-start.3 = ((f32[8,128,256]{2,1,0:T(8,128)}), f32[8,128,256]{2,1,0:T(8,128)S(1)}, u32[]{:S(2)}, u32[]{:S(2)}) async-start(f32[8,128,256]{2,1,0:T(8,128)} %stack.39), calls=%async_computation.3 | async-start | bytes 2097152 | tf_op jit(solution)/shard_map/all_to_all | solution.py:12
Sparse Core Ops, SparseCore 0:
  18.2 148.1 all-reduce.4
  195.3 21.7 all-gather.3
  221.2 144.9 all-reduce.6
  395.2 21.7 all-gather.5
  421.0 144.9 all-reduce.8
  596.0 21.7 all-gather.7
  621.9 144.9 all-reduce.10
